TPU v7x, 256 devices: a whole 4x4x8 slice. The times are simulated.
256 devices in a mesh: seq: 8 (over y, core), fsdp: 16 (over z_hi, x), tp: 2 (over z_lo).
Axes of the slice: x: 4, y: 4, z: 8 (z_hi: 4, z_lo: 2; z = z_hi * 2 + z_lo), core: 2. Of those that a mesh axis runs over, the one named last changes fastest.
Arguments:
- hidden: bfloat16 [16, 1024, 8192], P('fsdp', 'seq'), may hold values from -6 to 6
- queries: bfloat16 [16, 1024, 8192], P('fsdp', 'seq', 'tp'), may hold values from -600 to 600
- w_kv: bfloat16 [2, 8192, 1024], P(None, 'fsdp', 'tp'), may hold values from -0.0625 to 0.0625
- b_kv: bfloat16 [2, 1024], P(None, 'tp'), may hold values from -3 to 3
- doc_starts: int32 [16, 2], P('fsdp'), may hold values from 0 to 896, as said below
- block_docs: int32 [16, 8], P('fsdp'), may hold values from 0 to 1, as said below
Outputs:
- attended: bfloat16 [16, 1024, 8192], P('fsdp', 'seq', 'tp')
Inputs may be any that keep to these rules, and one draw needn't show every extreme that they name: `doc_starts`: each row holds exactly 2 documents of whole blocks of 128 tokens, starts rising from 0; one document of each row has exactly 6 blocks. `block_docs`: the document of each block, matching doc_starts.
All inputs are finite; a program needn't handle non-finite values.
Results may differ from a plain program's by a relative error of at most 0.015.
Values may be sent and summed in bfloat16 or wider, within the bound.
A program may use at most 128 MiB of HBM per device.

v0:
```python
import jax
import jax.numpy as jnp
from jax import lax
from jax.sharding import PartitionSpec as P

HD = 128
BLK = 128


def rotate_keys(key_heads, positions):
    half = key_heads.shape[-1] // 2
    freqs = jnp.exp(
        -jnp.arange(half, dtype=jnp.float32)
        * (2.0 / key_heads.shape[-1])
        * jnp.log(jnp.float32(1000000.0))
    )
    angle = positions.astype(jnp.float32)[:, None] * freqs[None, :]
    cosine = jnp.cos(angle)[:, None, :]
    sine = jnp.sin(angle)[:, None, :]
    first = key_heads[..., :half]
    second = key_heads[..., half:]
    return jnp.concatenate(
        [first * cosine - second * sine, second * cosine + first * sine], axis=-1
    )


def lookup_docs(token_index, block_table):
    block_index = token_index // BLK
    matches = block_index[:, None] == jnp.arange(block_table.shape[0], dtype=jnp.int32)[None, :]
    return jnp.sum(jnp.where(matches, block_table[None, :], 0), axis=1)


def per_device(hidden, queries, w_kv, b_kv, doc_starts, block_docs):
    tok_count = hidden.shape[1]
    own_rows = hidden[0]
    seq_pos = lax.axis_index("seq") * tok_count + jnp.arange(tok_count, dtype=jnp.int32)
    key_value = jnp.einsum(
        "td,cde->cte",
        own_rows,
        lax.all_gather(w_kv, "fsdp", axis=1, tiled=True),
        preferred_element_type=jnp.float32,
    )
    key_value = key_value + b_kv.astype(jnp.float32)[:, None, :]
    query_docs = lookup_docs(seq_pos, block_docs[0])
    doc_match = query_docs[:, None] == jnp.arange(doc_starts.shape[1], dtype=jnp.int32)[None, :]
    doc_first = jnp.sum(jnp.where(doc_match, doc_starts[0][None, :], 0), axis=1)
    positions = seq_pos - doc_first
    key_heads = key_value.shape[2] // HD
    group = queries.shape[2] // HD // key_heads
    rotated = rotate_keys(key_value[0].reshape(tok_count, key_heads, HD), positions)
    keys = rotated.astype(jnp.bfloat16).reshape(tok_count, key_heads * HD)
    values = key_value[1].astype(jnp.bfloat16)
    stacked = jnp.stack([keys, values])
    query_heads = queries[0].reshape(tok_count, key_heads, group, HD)
    inv_root = 1.0 / jnp.sqrt(jnp.float32(HD))
    piece = lax.all_gather(stacked, "seq", axis=1, tiled=True)
    width = piece.shape[1]
    key_docs = lookup_docs(jnp.arange(width, dtype=jnp.int32), block_docs[0])
    same_doc = query_docs[:, None] == key_docs[None, :]
    run_max = jnp.full((key_heads, group, tok_count), -1e30, jnp.float32)
    key_part = piece[0].reshape(width, key_heads, HD)
    value_part = piece[1].reshape(width, key_heads, HD)
    scores = (
        jnp.einsum("tgjd,sgd->gjts", query_heads, key_part, preferred_element_type=jnp.float32)
        * inv_root
    )
    scores = jnp.where(same_doc[None, None], scores, jnp.float32(-1e30))
    new_max = jnp.maximum(run_max, jnp.max(scores, axis=-1))
    weight = jnp.where(same_doc[None, None], jnp.exp(scores - new_max[..., None]), jnp.float32(0.0))
    new_sum = jnp.sum(weight, axis=-1)
    update = jnp.einsum(
        "gjts,sgd->gjtd",
        weight.astype(jnp.bfloat16),
        value_part,
        preferred_element_type=jnp.float32,
    )
    result = update / new_sum[..., None]
    result = jnp.transpose(result, (2, 0, 1, 3)).reshape(tok_count, key_heads * group * HD)
    return result.astype(jnp.bfloat16)[None]


def solution(mesh):
    in_specs = (
        P("fsdp", "seq", None),
        P("fsdp", "seq", "tp"),
        P(None, "fsdp", "tp"),
        P(None, "tp"),
        P("fsdp", None),
        P("fsdp", None),
    )
    out_specs = P("fsdp", "seq", "tp")
    return jax.shard_map(
        per_device, mesh=mesh, in_specs=in_specs, out_specs=out_specs, check_vma=False
    )
```

profile of v0, /device:TPU:1, one launch (start us, length us, event | category | flops | bytes accessed | tf_op | source)
XLA Modules:
  0.0 282.8 jit_solution(4501441677617884794)
XLA Ops:
  6.5 0.0 copy-start
  6.5 0.0 copy-start.1
  6.5 0.0 all-gather.3.cloned.1.call-start
  6.5 2.4 copy.12
  9.0 0.0 all-gather.3.cloned.1.call-update
  9.0 0.0 all-gather.5.cloned.1.call-start
  9.0 0.7 convert_element_type.39
  9.8 0.7 select_reduce_fusion.1
  10.5 0.7 fusion.22
  11.2 0.2 multiply_cosine_fusion
  11.4 211.2 %all-gather.3.cloned.1.call-done = bf16[2,8192,512]{1,2,0:T(8,128)(2,1)} async-done(((bf16[2,512,512]{1,2,0:T(8,128)(2,1)}), bf16[2,8192,512]{1,2,0:T(8,128)(2,1)}) %all-gather.3.cloned.1.call-update) | async-done | bytes 16777232 | tf_op jit(solution)/shard_map/all_gather | solution.py:40
  222.6 0.0 copy-done
  222.6 8.3 %fusion.14 = f32[2,128,512]{1,2,0:T(8,128)S(1)} fusion(bf16[2,8192,512]{1,2,0:T(8,128)(2,1)} %all-gather.3.cloned.1.call-done, bf16[1,128,8192]{2,1,0:T(8,128)(2,1)S(1)} %copy-done, f32[2,512]{1,0:T(2,128)S(1)} %convert_element_type.39), kind=kOutput, calls=%fused_computation.12 | convolution fusion | flops 2147614720 | bytes 19402752 | tf_op jit(solution)/shard_map/td,cde->cte/dot_general | solution.py:37
  231.0 0.7 pad_maximum_fusion
  231.8 0.0 all-gather.5.cloned.1.call-update
  231.8 1.5 copy.22
  233.3 0.0 copy-done.1
  233.3 0.1 select_reduce_fusion
  233.4 0.2 broadcast_compare_fusion
  233.6 27.8 %all-gather.5.cloned.1.call-done = bf16[2,1024,512]{1,2,0:T(8,128)(2,1)} async-done(((bf16[2,128,512]{1,2,0:T(8,128)(2,1)}), bf16[2,1024,512]{1,2,0:T(8,128)(2,1)}) %all-gather.5.cloned.1.call-update) | async-done | bytes 2097168 | tf_op jit(solution)/shard_map/all_gather | solution.py:56
  261.4 1.7 fusion.26
  263.1 3.0 %fusion = (f32[4,8,128]{2,1,0:T(8,128)S(1)}, f32[4,1024,128,8]{2,1,3,0:T(8,128)S(1)}) fusion(pred[128,1024]{0,1:T(8,128)(4,1)S(1)} %broadcast_compare_fusion, bf16[1024,4,128,1]{0,2,3,1:T(8,128)(2,1)S(1)} %bitcast.51, bf16[128,4,8,128]{3,2,1,0:T(8,128)(2,1)S(1)} %bitcast.50), kind=kOutput, calls=%fused_computation.2 | convolution fusion | flops 1086320640 | bytes 19021824 | tf_op jit(solution)/shard_map/tgjd,sgd->gjts/dot_general | solution.py:64
  266.1 4.1 %fusion.1 = f32[4,8,128]{2,1,0:T(8,128)S(1)} fusion(f32[4,1024,128,8]{2,1,3,0:T(8,128)S(1)} %get-tuple-element.12, f32[4,8,128]{2,1,0:T(8,128)S(1)} %broadcast_maximum_fusion, pred[128,1024]{0,1:T(8,128)(4,1)S(1)} %broadcast_compare_fusion), kind=kLoop, calls=%fused_computation.3 | loop fusion | flops 20967424 | bytes 16941056 | tf_op jit(solution)/shard_map/reduce_sum | solution.py:70
  270.3 4.3 %fusion.6 = bf16[128,4,8,128]{0,3,2,1:T(8,128)(2,1)S(1)} fusion(bf16[1024,4,128,1]{0,2,3,1:T(8,128)(2,1)S(1)} %bitcast.55, f32[4,1024,128,8]{2,1,3,0:T(8,128)S(1)} %get-tuple-element.12, f32[4,8,128]{2,1,0:T(8,128)S(1)} %broadcast_maximum_fusion, pred[128,1024]{0,1:T(8,128)(4,1)S(1)} %broadcast_compare_fusion, f32[128,4,8]{0,2,1:T(8,128)S(1)} %bitcast.57), kind=kOutput, calls=%fused_computation.8 | convolution fusion | flops 1095761920 | bytes 19038208 | tf_op jit(solution)/shard_map/gjts,sgd->gjtd/dot_general | solution.py:71
  274.6 1.3 copy.16
  (9 shorter events, 0.1 us)
Async XLA Ops:
  6.5 216.1 %copy-start = (bf16[1,128,8192]{2,1,0:T(8,128)(2,1)S(1)}, bf16[1,128,8192]{2,1,0:T(8,128)(2,1)}, u32[]{:S(2)}) copy-start(bf16[1,128,8192]{2,1,0:T(8,128)(2,1)} %param.6) | copy-start | bytes 6291460
  6.5 226.7 %copy-start.1 = (s32[1,8]{1,0:T(1,128)S(1)}, s32[1,8]{1,0:T(1,128)}, u32[]{:S(2)}) copy-start(s32[1,8]{1,0:T(1,128)} %param.11) | copy-start | bytes 100
  6.5 216.1 %all-gather.3.cloned.1.call-start = ((), (), s32[]{:S(2)}) async-start(), calls=%async_computation | async-start | bytes 17825792 | tf_op jit(solution)/shard_map/all_gather | solution.py:40
  9.0 252.4 %all-gather.5.cloned.1.call-start = ((), (), s32[]{:S(2)}) async-start(), calls=%async_computation.1 | async-start | bytes 2359296 | tf_op jit(solution)/shard_map/all_gather | solution.py:56
Sparse Core Ops, SparseCore 0:
  9.7 212.8 all-gather.2
  231.9 29.4 all-gather.4
where the time goes:
time: 283 us
  waiting for transfers between devices  239 us (84%)
  matrix products  15.6 us (6%)
  between operations  13.5 us (5%)
  other arithmetic  7.58 us (3%)
  local copies, waits for them, and re-layouts  6.95 us (2%)
    all_gather x1, waiting for transfers between devices, per_device(): lax.all_gather(w_kv, 'fsdp', axis=1, tiled=True)  211 us
    all_gather x1, waiting for transfers between devices, per_device(): piece = lax.all_gather(stacked, 'seq', axis=1, tiled=True)  27.8 us
    dot_general x1, matrix products, per_device(): jnp.einsum('td,cde->cte', own_rows, lax.all_gather(w_kv, 'fsdp', axis=1,...  8.31 us
  transfers between devices with their start and end apart: 2, of which 2 were waited for; matrix products, arithmetic and copies ran while one was open for 1% of the time, Pallas kernels for 0%

commit v1 on v0

v1 whole, which is shorter than its diff:
```python
import jax
import jax.numpy as jnp
from jax import lax
from jax.sharding import Mesh
from jax.sharding import PartitionSpec as P

HD = 128
BLK = 128

SEQ = ("sy", "sc")
FSDP = ("fz", "fx")


def rotate_keys(key_heads, positions):
    half = key_heads.shape[-1] // 2
    freqs = jnp.exp(
        -jnp.arange(half, dtype=jnp.float32)
        * (2.0 / key_heads.shape[-1])
        * jnp.log(jnp.float32(1000000.0))
    )
    angle = positions.astype(jnp.float32)[:, None] * freqs[None, :]
    cosine = jnp.cos(angle)[:, None, :]
    sine = jnp.sin(angle)[:, None, :]
    first = key_heads[..., :half]
    second = key_heads[..., half:]
    return jnp.concatenate(
        [first * cosine - second * sine, second * cosine + first * sine], axis=-1
    )


def lookup_docs(token_index, block_table):
    block_index = token_index // BLK
    matches = block_index[:, None] == jnp.arange(block_table.shape[0], dtype=jnp.int32)[None, :]
    return jnp.sum(jnp.where(matches, block_table[None, :], 0), axis=1)


def doc_positions(token_index, doc_starts, block_docs):
    docs = lookup_docs(token_index, block_docs[0])
    doc_match = docs[:, None] == jnp.arange(doc_starts.shape[1], dtype=jnp.int32)[None, :]
    doc_first = jnp.sum(jnp.where(doc_match, doc_starts[0][None, :], 0), axis=1)
    return docs, token_index - doc_first


def make_per_device(cores):
    def per_device(hidden, queries, w_kv, b_kv, doc_starts, block_docs):
        tok_count = hidden.shape[1]
        core = lax.axis_index("sc")
        chip = lax.axis_index("sy")
        cols = w_kv.shape[2] // cores
        w_part = lax.dynamic_slice_in_dim(w_kv, core * cols, cols, axis=2)
        b_part = lax.dynamic_slice_in_dim(b_kv, core * cols, cols, axis=1)
        chip_rows = lax.all_gather(hidden[0], "sc", axis=0, tiled=True)
        chip_tokens = chip_rows.shape[0]
        key_value = jnp.einsum(
            "td,cde->cte",
            chip_rows,
            lax.all_gather(w_part, FSDP, axis=1, tiled=True),
            preferred_element_type=jnp.float32,
        )
        key_value = key_value + b_part.astype(jnp.float32)[:, None, :]
        chip_pos = chip * chip_tokens + jnp.arange(chip_tokens, dtype=jnp.int32)
        _, positions = doc_positions(chip_pos, doc_starts, block_docs)
        part_heads = cols // HD
        rotated = rotate_keys(key_value[0].reshape(chip_tokens, part_heads, HD), positions)
        keys = rotated.astype(jnp.bfloat16).reshape(chip_tokens, cols)
        values = key_value[1].astype(jnp.bfloat16)
        stacked = jnp.stack([keys, values])
        gathered = lax.all_gather(stacked, SEQ, axis=0, tiled=False)
        chips = gathered.shape[0] // cores
        gathered = gathered.reshape(chips, cores, 2, chip_tokens, cols)
        piece = jnp.transpose(gathered, (2, 0, 3, 1, 4)).reshape(2, chips * chip_tokens, cores * cols)

        seq_pos = (chip * cores + core) * tok_count + jnp.arange(tok_count, dtype=jnp.int32)
        query_docs = lookup_docs(seq_pos, block_docs[0])
        key_heads = piece.shape[2] // HD
        group = queries.shape[2] // HD // key_heads
        query_heads = queries[0].reshape(tok_count, key_heads, group, HD)
        inv_root = 1.0 / jnp.sqrt(jnp.float32(HD))
        width = piece.shape[1]
        key_docs = lookup_docs(jnp.arange(width, dtype=jnp.int32), block_docs[0])
        same_doc = query_docs[:, None] == key_docs[None, :]
        run_max = jnp.full((key_heads, group, tok_count), -1e30, jnp.float32)
        key_part = piece[0].reshape(width, key_heads, HD)
        value_part = piece[1].reshape(width, key_heads, HD)
        scores = (
            jnp.einsum("tgjd,sgd->gjts", query_heads, key_part, preferred_element_type=jnp.float32)
            * inv_root
        )
        scores = jnp.where(same_doc[None, None], scores, jnp.float32(-1e30))
        new_max = jnp.maximum(run_max, jnp.max(scores, axis=-1))
        weight = jnp.where(same_doc[None, None], jnp.exp(scores - new_max[..., None]), jnp.float32(0.0))
        new_sum = jnp.sum(weight, axis=-1)
        update = jnp.einsum(
            "gjts,sgd->gjtd",
            weight.astype(jnp.bfloat16),
            value_part,
            preferred_element_type=jnp.float32,
        )
        result = update / new_sum[..., None]
        result = jnp.transpose(result, (2, 0, 1, 3)).reshape(tok_count, key_heads * group * HD)
        return result.astype(jnp.bfloat16)[None]

    return per_device


def solution(mesh):
    seq, fsdp, tp = (mesh.shape[name] for name in ("seq", "fsdp", "tp"))
    cores = 2
    x_size = 4
    fine = Mesh(
        mesh.devices.reshape(seq // cores, cores, fsdp // x_size, x_size, tp),
        ("sy", "sc", "fz", "fx", "tp"),
    )
    in_specs = (
        P(FSDP, SEQ, None),
        P(FSDP, SEQ, "tp"),
        P(None, FSDP, "tp"),
        P(None, "tp"),
        P(FSDP, None),
        P(FSDP, None),
    )
    out_specs = P(FSDP, SEQ, "tp")
    return jax.shard_map(
        make_per_device(cores), mesh=fine, in_specs=in_specs, out_specs=out_specs, check_vma=False
    )
```

time: 283 us -> 223 us (0.79)
  waiting for transfers between devices: 239 us -> 173 us
  local copies, waits for them, and re-layouts: 6.95 us -> 13.9 us
    all_gather x2 -> x3, waiting for transfers between devices: 239 us -> 173 us  [the longest x1 127 us: per_device(): lax.all_gather(w_part, FSDP, axis=1, tiled=True)]
    another operation x0 -> x3, local copies, waits for them, and re-layouts: none -> 4.44 us  [the longest x1 1.79 us: per_device(): key_part = piece[0].reshape(width, key_heads, HD)]
    reshape x0 -> x1, local copies, waits for them, and re-layouts: none -> 3.06 us  [per_device(): gathered = gathered.reshape(chips, cores, 2, chip_tokens, cols)]
  transfers between devices with their start and end apart: 2 -> 3, of which waited for: 2 -> 3; matrix products, arithmetic and copies ran while one was open for 1% -> 2% of each run, Pallas kernels for 0% -> 0%
where the time goes in v1:
time: 223 us
  waiting for transfers between devices  173 us (78%)
  matrix products  15.3 us (7%)
  local copies, waits for them, and re-layouts  13.9 us (6%)
  between operations  13.3 us (6%)
  other arithmetic  7.09 us (3%)
    all_gather x1, waiting for transfers between devices, per_device(): lax.all_gather(w_part, FSDP, axis=1, tiled=True)  127 us
    all_gather x1, waiting for transfers between devices, per_device(): gathered = lax.all_gather(stacked, SEQ, axis=0, tiled=False)  24.6 us
    all_gather x1, waiting for transfers between devices, per_device(): chip_rows = lax.all_gather(hidden[0], 'sc', axis=0, tiled=True)  21 us
    dot_general x1, matrix products, per_device(): jnp.einsum('td,cde->cte', chip_rows, lax.all_gather(w_part, FSDP, axis=1,...  6.93 us
  transfers between devices with their start and end apart: 3, of which 3 were waited for; matrix products, arithmetic and copies ran while one was open for 2% of the time, Pallas kernels for 0%

profile of v1, /device:TPU:1, one launch (start us, length us, event | category | flops | bytes accessed | tf_op | source)
XLA Modules:
  0.0 223.2 jit_solution(64430388502400549)
XLA Ops:
  6.5 0.0 copy-start
  6.5 0.0 all-gather.8.cloned.1.call-start
  6.5 0.7 all-gather.8.cloned.1.call-update
  7.3 0.0 all-gather.6.cloned.1.call-start
  7.3 0.8 copy-done
  8.1 1.0 copy.37
  9.1 0.0 all-gather.6.cloned.1.call-update
  9.1 0.0 all-gather.10.cloned.1.call-start
  9.2 0.7 dynamic-slice_convert_fusion
  9.9 0.7 select_reduce_fusion.1
  10.7 0.7 fusion.24
  11.4 0.3 multiply_cosine_fusion
  11.7 21.0 %all-gather.8.cloned.1.call-done = bf16[1,256,8192]{2,1,0:T(8,128)(2,1)} async-done(((bf16[1,128,8192]{2,1,0:T(8,128)(2,1)}), bf16[1,256,8192]{2,1,0:T(8,128)(2,1)}) %all-gather.8.cloned.1.call-update) | async-done | bytes 4194320 | tf_op jit(solution)/shard_map/all_gather | solution.py:52
  32.7 127.1 %all-gather.6.cloned.1.call-done = bf16[2,8192,256]{1,2,0:T(8,128)(2,1)} async-done(((bf16[2,512,256]{1,2,0:T(8,128)(2,1)}), bf16[2,8192,256]{1,2,0:T(8,128)(2,1)}) %all-gather.6.cloned.1.call-update) | async-done | bytes 8388624 | tf_op jit(solution)/shard_map/all_gather | solution.py:57
  159.8 6.9 %fusion.14 = f32[2,256,256]{1,2,0:T(8,128)S(1)} fusion(bf16[2,8192,256]{1,2,0:T(8,128)(2,1)} %all-gather.6.cloned.1.call-done, bf16[1,256,8192]{2,1,0:T(8,128)(2,1)} %all-gather.8.cloned.1.call-done, f32[2,256]{1,0:T(2,128)S(1)} %dynamic-slice_convert_fusion), kind=kOutput, calls=%fused_computation.12 | convolution fusion | flops 2147614720 | bytes 13109248 | tf_op jit(solution)/shard_map/td,cde->cte/dot_general | solution.py:54
  166.9 0.9 copy.26
  167.8 0.0 all-gather.10.cloned.1.call-update
  167.8 0.0 copy-done.1
  167.8 1.2 copy.38
  169.0 0.0 copy-done.2
  169.0 0.1 select_reduce_fusion.2
  169.1 0.1 select_reduce_fusion
  169.2 0.2 broadcast_compare_fusion
  169.4 24.6 %all-gather.10.cloned.1.call-done = bf16[16,256,256]{2,1,0:T(8,128)(2,1)} async-done(((bf16[2,256,256]{2,1,0:T(8,128)(2,1)}), bf16[16,256,256]{2,1,0:T(8,128)(2,1)}) %all-gather.10.cloned.1.call-update) | async-done | bytes 2097168 | tf_op jit(solution)/shard_map/all_gather | solution.py:68
  194.0 3.1 %copy.27 = bf16[4,2,2,256,256]{3,0,4,1,2:T(4,128)(2,1)S(1)} copy(bf16[4,2,2,256,256]{4,3,2,1,0:T(8,128)(2,1)} %bitcast.56) | data formatting | bytes 4194304 | tf_op jit(solution)/shard_map/reshape | solution.py:70
  197.1 2.1 fusion.28
  199.2 1.8 reshape.180
  201.0 1.8 reshape_squeeze.13
  202.8 4.1 %fusion = (f32[4,8,128]{2,1,0:T(8,128)S(1)}, f32[4,1024,128,8]{2,1,3,0:T(8,128)S(1)}) fusion(pred[128,1024]{0,1:T(8,128)(4,1)S(1)} %broadcast_compare_fusion, bf16[128,4,8,128]{3,2,1,0:T(8,128)(2,1)} %bitcast.55, bf16[1024,4,128]{0,2,1:T(8,128)(2,1)S(1)} %reshape_squeeze.13), kind=kOutput, calls=%fused_computation.2 | convolution fusion | flops 1086320640 | bytes 19021824 | tf_op jit(solution)/shard_map/tgjd,sgd->gjts/dot_general | solution.py:86
  206.9 4.1 %fusion.1 = f32[4,8,128]{2,1,0:T(8,128)S(1)} fusion(f32[4,1024,128,8]{2,1,3,0:T(8,128)S(1)} %get-tuple-element.12, f32[4,8,128]{2,1,0:T(8,128)S(1)} %broadcast_maximum_fusion, pred[128,1024]{0,1:T(8,128)(4,1)S(1)} %broadcast_compare_fusion), kind=kLoop, calls=%fused_computation.3 | loop fusion | flops 20967424 | bytes 16941056 | tf_op jit(solution)/shard_map/reduce_sum | solution.py:92
  211.0 4.3 %fusion.8 = bf16[128,4,8,128]{0,3,2,1:T(8,128)(2,1)S(1)} fusion(f32[4,1024,128,8]{2,1,3,0:T(8,128)S(1)} %get-tuple-element.12, f32[4,8,128]{2,1,0:T(8,128)S(1)} %broadcast_maximum_fusion, pred[128,1024]{0,1:T(8,128)(4,1)S(1)} %broadcast_compare_fusion, bf16[1024,4,128,1]{0,2,1,3:T(8,128)(2,1)S(1)} %reshape.180, f32[128,4,8]{0,2,1:T(8,128)S(1)} %bitcast.61), kind=kOutput, calls=%fused_computation.10 | convolution fusion | flops 1095761920 | bytes 19038208 | tf_op jit(solution)/shard_map/gjts,sgd->gjtd/dot_general | solution.py:93
  215.4 1.3 copy.31
  (14 shorter events, 0.2 us)
Async XLA Ops:
  6.5 1.5 copy-start
  6.5 162.5 %copy-start.2 = (s32[1,8]{1,0:T(1,128)S(1)}, s32[1,8]{1,0:T(1,128)}, u32[]{:S(2)}) copy-start(s32[1,8]{1,0:T(1,128)} %param.11) | copy-start | bytes 100
  6.5 161.3 %copy-start.1 = (bf16[1,128,4096]{2,1,0:T(8,128)(2,1)S(1)}, bf16[1,128,4096]{2,1,0:T(8,128)(2,1)}, u32[]{:S(2)}) copy-start(bf16[1,128,4096]{2,1,0:T(8,128)(2,1)} %param.7) | copy-start | bytes 3145732
  6.5 26.1 %all-gather.8.cloned.1.call-start = ((), (), s32[]{:S(2)}) async-start(), calls=%async_computation.1 | async-start | bytes 6291456 | tf_op jit(solution)/shard_map/all_gather | solution.py:52
  7.3 152.5 %all-gather.6.cloned.1.call-start = ((), (), s32[]{:S(2)}) async-start(), calls=%async_computation | async-start | bytes 8912896 | tf_op jit(solution)/shard_map/all_gather | solution.py:57
  9.1 184.9 %all-gather.10.cloned.1.call-start = ((), (), s32[]{:S(2)}) async-start(), calls=%async_computation.2 | async-start | bytes 2359296 | tf_op jit(solution)/shard_map/all_gather | solution.py:68
Sparse Core Ops, SparseCore 0:
  9.1 23.5 all-gather.7
  35.1 124.6 all-gather.5
  167.9 26.0 all-gather.9

commit v2 on v1

--- a/solution.py
+++ b/solution.py
@@ -49,7 +49,13 @@
         cols = w_kv.shape[2] // cores
         w_part = lax.dynamic_slice_in_dim(w_kv, core * cols, cols, axis=2)
         b_part = lax.dynamic_slice_in_dim(b_kv, core * cols, cols, axis=1)
-        chip_rows = lax.all_gather(hidden[0], "sc", axis=0, tiled=True)
+        own_rows = hidden[0]
+        partner_rows = lax.ppermute(own_rows, "sc", [(i, (i + 1) % cores) for i in range(cores)])
+        chip_rows = jnp.where(
+            core == 0,
+            jnp.concatenate([own_rows, partner_rows]),
+            jnp.concatenate([partner_rows, own_rows]),
+        )
         chip_tokens = chip_rows.shape[0]
         key_value = jnp.einsum(
             "td,cde->cte",

time: 223 us -> 203 us (0.910)
  waiting for transfers between devices: 173 us -> 148 us
  starting transfers between devices: 0.08 us -> 3.33 us
    all_gather x1 -> x0, waiting for transfers between devices: 21 us -> none  [per_device(): chip_rows = lax.all_gather(hidden[0], 'sc', axis=0, tiled=True)]
    all_gather x1, waiting for transfers between devices: 127 us -> 121 us  [per_device(): lax.all_gather(w_part, FSDP, axis=1, tiled=True)]
    ppermute x0 -> x1, starting transfers between devices: none -> 3.29 us  [per_device(): lax.ppermute(own_rows, 'sc', [(i, (i + 1) % cores) for i in range(cores)])]
where the time goes in v2:
time: 203 us
  waiting for transfers between devices  148 us (73%)
  matrix products  16.7 us (8%)
  local copies, waits for them, and re-layouts  14.4 us (7%)
  between operations  13.6 us (7%)
  other arithmetic  7.08 us (3%)
  starting transfers between devices  3.33 us (2%)
    all_gather x1, waiting for transfers between devices, per_device(): lax.all_gather(w_part, FSDP, axis=1, tiled=True)  121 us
    all_gather x1, waiting for transfers between devices, per_device(): gathered = lax.all_gather(stacked, SEQ, axis=0, tiled=False)  24.6 us
    dot_general x1, matrix products, per_device(): jnp.einsum('td,cde->cte', chip_rows, lax.all_gather(w_part, FSDP, axis=1,...  8.26 us
    dot_general x1, matrix products, per_device(): jnp.einsum('gjts,sgd->gjtd', weight.astype(jnp.bfloat16), value_part, pre...  4.34 us
    reduce_sum x1, other arithmetic, per_device(): new_sum = jnp.sum(weight, axis=-1)  4.12 us
    dot_general x1, matrix products, per_device(): jnp.einsum('tgjd,sgd->gjts', query_heads, key_part, preferred_element_typ...  4.07 us
  transfers between devices with their start and end apart: 3, of which 3 were waited for; matrix products, arithmetic and copies ran while one was open for 2% of the time, Pallas kernels for 0%

profile of v2, /device:TPU:1, one launch (start us, length us, event | category | flops | bytes accessed | tf_op | source)
XLA Modules:
  0.0 202.7 jit_solution(13124850213616513827)
XLA Ops:
  6.5 0.0 copy-start
  6.5 0.0 all-gather.4.cloned.1.call-start
  6.5 1.2 copy-done
  7.8 1.0 copy.37
  8.8 0.0 all-gather.4.cloned.1.call-update
  8.8 0.0 all-gather.6.cloned.1.call-start
  8.9 3.3 %collective-permute-start = (bf16[128,8192]{1,0:T(8,128)(2,1)}, bf16[128,8192]{1,0:T(8,128)(2,1)}, u32[]{:S(2)}, u32[]{:S(2)}) collective-permute-start(bf16[128,8192]{1,0:T(8,128)(2,1)} %bitcast.66), channel_id=1, source_target_pairs={{0,32},{32,0},{1,33},{33,1},{2,34},{34,2},{3,35},{35,3},{4,36},{36... | collective-permute-start | bytes 6291464 | tf_op jit(solution)/shard_map/ppermute | solution.py:53
  12.2 0.7 dynamic-slice_convert_fusion
  12.9 0.7 select_reduce_fusion.1
  13.6 0.7 fusion.31
  14.4 0.3 multiply_cosine_fusion
  14.7 0.0 copy-start.1
  14.7 0.0 copy-start.2
  14.7 1.6 collective-permute-done
  16.3 121.4 %all-gather.4.cloned.1.call-done = bf16[2,8192,256]{1,2,0:T(8,128)(2,1)} async-done(((bf16[2,512,256]{1,2,0:T(8,128)(2,1)}), bf16[2,8192,256]{1,2,0:T(8,128)(2,1)}) %all-gather.4.cloned.1.call-update) | async-done | bytes 8388624 | tf_op jit(solution)/shard_map/all_gather | solution.py:63
  137.7 8.3 %fusion.21 = f32[2,256,256]{1,2,0:T(8,128)S(1)} fusion(bf16[2,8192,256]{1,2,0:T(8,128)(2,1)} %all-gather.4.cloned.1.call-done, bf16[128,8192]{1,0:T(8,128)(2,1)} %collective-permute-done, bf16[128,8192]{1,0:T(8,128)(2,1)} %bitcast.67, pred[]{:T(512)S(6)} %eq.81, f32[2,256]{1,0:T(2,128)S(1)} %dynamic-slice_convert_fusion), kind=kOutput, calls=%fused_computation.19 | convolution fusion | flops 2166489088 | bytes 13109249 | tf_op jit(solution)/shard_map/td,cde->cte/dot_general | solution.py:60
  146.1 0.9 copy.26
  147.0 0.0 all-gather.6.cloned.1.call-update
  147.0 1.2 copy.38
  148.2 0.0 copy-done.2
  148.2 0.1 select_reduce_fusion.2
  148.3 0.1 select_reduce_fusion
  148.4 0.2 broadcast_compare_fusion
  148.6 24.6 %all-gather.6.cloned.1.call-done = bf16[16,256,256]{2,1,0:T(8,128)(2,1)} async-done(((bf16[2,256,256]{2,1,0:T(8,128)(2,1)}), bf16[16,256,256]{2,1,0:T(8,128)(2,1)}) %all-gather.6.cloned.1.call-update) | async-done | bytes 2097168 | tf_op jit(solution)/shard_map/all_gather | solution.py:74
  173.2 3.1 %copy.27 = bf16[4,2,2,256,256]{3,0,4,1,2:T(4,128)(2,1)S(1)} copy(bf16[4,2,2,256,256]{4,3,2,1,0:T(8,128)(2,1)} %bitcast.56) | data formatting | bytes 4194304 | tf_op jit(solution)/shard_map/reshape | solution.py:76
  176.3 2.1 %fusion.36 = (bf16[1,4,256,2,256]{2,1,4,3,0:T(4,128)(2,1)}, bf16[1,4,256,2,256]{2,1,4,3,0:T(4,128)(2,1)}) fusion(bf16[2,4,256,2,256]{2,1,4,3,0:T(4,128)(2,1)S(1)} %bitcast.54), kind=kLoop, calls=%fused_computation.65 | loop fusion | bytes 4194304 | tf_op jit(solution)/shard_map/slice | solution.py:90
  178.4 1.8 reshape.179
  180.2 1.8 reshape_squeeze.13
  182.0 4.1 %fusion = (f32[4,8,128]{2,1,0:T(8,128)S(1)}, f32[4,1024,128,8]{2,1,3,0:T(8,128)S(1)}) fusion(pred[128,1024]{0,1:T(8,128)(4,1)S(1)} %broadcast_compare_fusion, bf16[128,4,8,128]{3,2,1,0:T(8,128)(2,1)} %bitcast.55, bf16[1024,4,128]{0,2,1:T(8,128)(2,1)S(1)} %reshape_squeeze.13), kind=kOutput, calls=%fused_computation.2 | convolution fusion | flops 1086320640 | bytes 19021824 | tf_op jit(solution)/shard_map/tgjd,sgd->gjts/dot_general | solution.py:92
  186.1 4.1 %fusion.1 = f32[4,8,128]{2,1,0:T(8,128)S(1)} fusion(f32[4,1024,128,8]{2,1,3,0:T(8,128)S(1)} %get-tuple-element.12, f32[4,8,128]{2,1,0:T(8,128)S(1)} %broadcast_maximum_fusion, pred[128,1024]{0,1:T(8,128)(4,1)S(1)} %broadcast_compare_fusion), kind=kLoop, calls=%fused_computation.3 | loop fusion | flops 20967424 | bytes 16941056 | tf_op jit(solution)/shard_map/reduce_sum | solution.py:98
  190.2 4.3 %fusion.15 = bf16[128,4,8,128]{0,3,2,1:T(8,128)(2,1)S(1)} fusion(f32[4,1024,128,8]{2,1,3,0:T(8,128)S(1)} %get-tuple-element.12, f32[4,8,128]{2,1,0:T(8,128)S(1)} %broadcast_maximum_fusion, pred[128,1024]{0,1:T(8,128)(4,1)S(1)} %broadcast_compare_fusion, bf16[1024,4,128,1]{0,2,1,3:T(8,128)(2,1)S(1)} %reshape.179, f32[128,4,8]{0,2,1:T(8,128)S(1)} %bitcast.61), kind=kOutput, calls=%fused_computation.17 | convolution fusion | flops 1095761920 | bytes 19038208 | tf_op jit(solution)/shard_map/gjts,sgd->gjtd/dot_general | solution.py:99
  194.5 1.3 copy.31
  (13 shorter events, 0.2 us)
Async XLA Ops:
  6.5 1.2 copy-start
  6.5 131.1 %all-gather.4.cloned.1.call-start = ((), (), s32[]{:S(2)}) async-start(), calls=%async_computation | async-start | bytes 8912896 | tf_op jit(solution)/shard_map/all_gather | solution.py:63
  8.8 164.4 %all-gather.6.cloned.1.call-start = ((), (), s32[]{:S(2)}) async-start(), calls=%async_computation.1 | async-start | bytes 2359296 | tf_op jit(solution)/shard_map/all_gather | solution.py:74
  8.9 7.4 %collective-permute-start = (bf16[128,8192]{1,0:T(8,128)(2,1)}, bf16[128,8192]{1,0:T(8,128)(2,1)}, u32[]{:S(2)}, u32[]{:S(2)}) collective-permute-start(bf16[128,8192]{1,0:T(8,128)(2,1)} %bitcast.66), channel_id=1, source_target_pairs={{0,32},{32,0},{1,33},{33,1},{2,34},{34,2},{3,35},{35,3},{4,36},{36... | collective-permute-start | bytes 6291464 | tf_op jit(solution)/shard_map/ppermute | solution.py:53
  14.7 132.3 %copy-start.1 = (bf16[1,128,4096]{2,1,0:T(8,128)(2,1)S(1)}, bf16[1,128,4096]{2,1,0:T(8,128)(2,1)}, u32[]{:S(2)}) copy-start(bf16[1,128,4096]{2,1,0:T(8,128)(2,1)} %param.7) | copy-start | bytes 3145732
  14.7 133.5 %copy-start.2 = (s32[1,8]{1,0:T(1,128)S(1)}, s32[1,8]{1,0:T(1,128)}, u32[]{:S(2)}) copy-start(s32[1,8]{1,0:T(1,128)} %param.11) | copy-start | bytes 100
Sparse Core Ops, SparseCore 0:
  9.7 127.8 all-gather.3
  147.1 26.0 all-gather.5
